TPU v7x, 32 devices: a whole 2x2x4 slice. The times are simulated.
32 devices in a mesh: pair: 2 (over y), src: 8 (over z, x), tgt: 2 (over core).
Axes of the slice: x: 2, y: 2, z: 4, core: 2. Of those that a mesh axis runs over, the one named last changes fastest.
Arguments:
- source_features: bfloat16 [64, 8, 256], P('pair', 'src'), parts along dimension 0, may hold values from -6 to 6
- target_features: bfloat16 [128, 8, 256], P(('pair', 'tgt'), 'src'), parts along dimension 0, may hold values from -6 to 6
- source_rows: int32 [8], P('pair'), parts along dimension 0, may hold values from 0 to 31
- target_cols: int32 [16], P('pair'), parts along dimension 0, may hold values from 0 to 7, each once
- target_kernel_one: bfloat16 [3, 3, 16, 16], replicated, may hold values from -0.75 to 0.75
- source_kernel: bfloat16 [3, 3, 16, 16], replicated, may hold values from -0.75 to 0.75
- target_kernel_two: bfloat16 [3, 3, 16, 16], replicated, may hold values from -0.75 to 0.75
Outputs:
- filtered: bfloat16 [8, 8, 64, 128], P('pair', 'src', 'tgt'), parts along dimension 0
There are 2 independent parts, one for each index of `pair`. A program takes and returns all parts, laid end to end along the dimension named above; an argument that names none is the same for every part. Nothing has to cross between parts.
Inputs may be any that keep to these rules, and one draw needn't show every extreme that they name: `target_cols`: each column index appears once.
All inputs are finite; a program needn't handle non-finite values.
Results may differ from a plain program's by a relative error of at most 0.0074.
Values may be sent and summed in bfloat16 or wider, within the bound.
No kernel may reach another device: no remote copies, remote signals or barrier semaphores. Data moves between devices by JAX's collectives and lax.ppermute only.
A program may use at most 128 MiB of HBM per device.

v0:
```python
import functools
import math

import jax
import jax.numpy as jnp
from jax import lax
from jax.experimental import pallas as pl
from jax.experimental.pallas import tpu as pltpu
from jax.sharding import PartitionSpec as P


LANES = 128
TILE = 8


def rounds_of(count):
    rounds = []
    while count > 4:
        count //= 2
        rounds.append([(count, count)])
    rounds.append([(1, 2), (2, 1), (3, 3)] if count == 4 else [(1, 1)])
    return rounds


def entries_of(count):
    *early, last = rounds_of(count)
    held = [(0, 0)]
    for ((mask, _),) in early:
        held = held + [(offset ^ mask, hops + 1) for offset, hops in held]
    entries = [(0, 0, k, (offset, offset), hops) for k, (offset, hops) in enumerate(held)]
    for part, (sent_0, sent_1) in enumerate(last):
        twin = last.index((sent_1, sent_0))
        entries += [
            (part + 1, twin + 1, k, (offset ^ sent_1, offset ^ sent_0), hops + 1)
            for k, (offset, hops) in enumerate(held)
        ]
    return entries


def pack_kernel(count, rows_hbm, source_hbm, target_hbm, *refs):
    kernels, (out_ref, *held), (rows_ref, source_ref, wide_ref, sems) = (
        refs[:count],
        refs[count : 2 * count + 1],
        refs[2 * count + 1 :],
    )
    rows = target_hbm.shape[0]
    window = rows_hbm.shape[0]
    copies = [
        pltpu.make_async_copy(source, target, sems.at[index])
        for index, (source, target) in enumerate(
            [
                (rows_hbm, rows_ref),
                (source_hbm, source_ref),
                (target_hbm, out_ref.at[0, pl.ds(0, rows)]),
                *zip(kernels, held, strict=True),
            ]
        )
    ]
    for copy in copies:
        copy.start()
    copies[1].wait()
    wide_ref[...] = source_ref[...].astype(jnp.float32)
    copies[0].wait()
    lines = [wide_ref[pl.ds(rows_ref[h], 1), :] for h in range(window)]
    blank = out_ref.shape[1] - rows - window
    if blank:
        lines.append(jnp.zeros((blank, wide_ref.shape[1]), jnp.float32))
    out_ref[0, rows:, :] = jnp.concatenate(lines, axis=0).astype(out_ref.dtype)
    for copy in copies[2:]:
        copy.wait()


def pack(source_rows, source, target, kernels, height):
    operands = (source_rows, source, target, *kernels)
    out, *held = pl.pallas_call(
        functools.partial(pack_kernel, len(kernels)),
        out_shape=[
            jax.ShapeDtypeStruct((1, height, target.shape[1]), target.dtype),
            *(jax.ShapeDtypeStruct(kernel.shape, kernel.dtype) for kernel in kernels),
        ],
        in_specs=[pl.BlockSpec(memory_space=pltpu.HBM)] * len(operands),
        out_specs=[pl.BlockSpec(memory_space=pltpu.VMEM)] * (1 + len(kernels)),
        scratch_shapes=[
            pltpu.SMEM(source_rows.shape, source_rows.dtype),
            pltpu.VMEM(source.shape, source.dtype),
            pltpu.VMEM(source.shape, jnp.float32),
            pltpu.SemaphoreType.DMA((3 + len(kernels),)),
        ],
        compiler_params=pltpu.CompilerParams(vmem_limit_bytes=4 << 20),
        name="pack",
    )(*(pltpu.with_memory_space_constraint(x, pltpu.HBM) for x in operands))
    return out, held


def widen(block):
    return jnp.concatenate(
        [
            block.astype(jnp.float32),
            jnp.zeros((block.shape[0], LANES - block.shape[1]), jnp.float32),
        ],
        axis=1,
    )


def band_rows(kernel_ref, a, place, breadth):
    groups = kernel_ref.shape[2]
    total = jnp.zeros((groups, LANES), jnp.float32)
    for b in range(3):
        out_place = place - b + 1
        if 0 <= out_place < breadth:
            piece = widen(kernel_ref[a, b])
            total = total + (pltpu.roll(piece, out_place * groups, 1) if out_place else piece)
    return total


def weights_kernel(offsets, cols_ref, one_ref, source_ref, two_ref, band_one, blocks, band_two):
    groups = one_ref.shape[2]
    breadth = LANES // groups
    here = lax.axis_index("src")
    first = lax.axis_index("tgt") == 0
    for place in range(breadth):
        offset = jnp.bitwise_xor(cols_ref[place], here)
        entry = 0
        for index, (on_0, on_1) in enumerate(offsets):
            entry = jnp.where(offset == jnp.where(first, on_0, on_1), index, entry)
        start = pl.multiple_of(entry * groups, groups)
        for a in range(3):
            lanes = slice(a * LANES, (a + 1) * LANES)
            band_one[pl.ds(start, groups), lanes] = band_rows(one_ref, a, place, breadth).astype(
                band_one.dtype
            )
            row = a * LANES + place * groups
            band_two[row : row + groups, :] = band_rows(two_ref, a, place, breadth).astype(
                band_two.dtype
            )
            for b in range(3):
                piece = widen(source_ref[a, b])
                piece = pltpu.roll(piece, place * groups, 1) if place else piece
                row = b * LANES + place * groups
                blocks[row : row + groups, lanes] = piece.astype(blocks.dtype)


def weights(target_cols, one, source, two, offsets):
    smem = pl.BlockSpec(memory_space=pltpu.SMEM)
    vmem = pl.BlockSpec(memory_space=pltpu.VMEM)
    return pl.pallas_call(
        functools.partial(weights_kernel, offsets),
        out_shape=[
            jax.ShapeDtypeStruct((LANES, 3 * LANES), one.dtype),
            jax.ShapeDtypeStruct((3 * LANES, 3 * LANES), one.dtype),
            jax.ShapeDtypeStruct((3 * LANES, LANES), one.dtype),
        ],
        in_specs=[smem, vmem, vmem, vmem],
        out_specs=[vmem, vmem, vmem],
        compiler_params=pltpu.CompilerParams(vmem_limit_bytes=4 << 20),
        name="weights",
    )(target_cols, one, source, two)


def shifted_sum(product):
    rows = product.shape[0]
    below = pltpu.roll(product[:, :LANES], 1, 0)
    above = pltpu.roll(product[:, 2 * LANES :], rows - 1, 0)
    return below + product[:, LANES : 2 * LANES] + above


def row_taps(plane):
    rows = plane.shape[0]
    return jnp.concatenate([pltpu.roll(plane, 1, 0), plane, pltpu.roll(plane, rows - 1, 0)], axis=1)


def swap_lane_groups(arrays, groups):
    lane_group = lax.broadcasted_iota(jnp.int32, arrays[0].shape, 1) // groups
    bit = len(arrays) // 2
    while bit:
        lower = (lane_group // bit) % 2 == 0
        result = list(arrays)
        for index in range(len(arrays)):
            if index & bit:
                continue
            low, high = arrays[index], arrays[index | bit]
            result[index] = jnp.where(lower, low, pltpu.roll(high, bit * groups, 1))
            result[index | bit] = jnp.where(lower, pltpu.roll(low, LANES - bit * groups, 1), high)
        arrays = result
        bit //= 2
    return arrays


def planes_of(product, count, planes, groups):
    rows = product.shape[0] // count
    result = []
    for start in range(0, planes, count):
        lanes = min(1 << (planes - start - 1).bit_length(), count)
        blocks = [
            product[entry * rows : (entry + 1) * rows, start * groups : (start + lanes) * groups]
            for entry in range(count)
        ]
        stack = [
            jnp.concatenate(blocks[low::lanes], axis=1) if lanes < count else blocks[low]
            for low in range(lanes)
        ]
        result += swap_lane_groups(stack, groups)[: planes - start]
    return result


def planes_padded(planes, count):
    left = planes % count
    return planes - left + (1 << (left - 1).bit_length() if left else 0)


class Block:
    def __init__(self, rows):
        self.rows = rows
        self.first = lax.axis_index("tgt") == 0
        self.outside_from = jnp.where(self.first, TILE - 2, 0)

    def beside(self, other):
        return jnp.where(
            self.first,
            other[: TILE, :].astype(jnp.float32),
            other[self.rows - TILE : self.rows, :].astype(jnp.float32),
        )

    def keep_inside(self, tiles):
        row = lax.broadcasted_iota(jnp.int32, tiles.shape, 0) % TILE
        outside = (row >= self.outside_from) & (row < self.outside_from + 2)
        return jnp.where(outside, 0.0, tiles)


def correlate(columns, spread, channels):
    product = lax.dot_general(
        columns, spread, (((1,), (1,)), ((), ())), preferred_element_type=jnp.float32
    )
    return product * channels ** (-0.5)


def volume_kernel(entries, groups, window, *refs):
    *parts, base_ref, edge_ref, spread_ref = refs
    count = len(entries)
    width = parts[0].shape[2]
    planes = 3 * window
    rows = base_ref.shape[0] // planes
    channels = width // groups
    here = lax.axis_index("src")
    block = Block(rows)
    first = block.first
    half = (len(parts) + 1) // 2
    near = [parts[part].at[k] for part, _, k, _, _ in entries]
    far = [
        parts[half + twin].at[k] if half + twin < len(parts) else parts[part].at[k]
        for part, twin, k, _, _ in entries
    ]

    def source_rows(entry):
        return near[entry][rows : rows + TILE, :].astype(jnp.float32)

    before = jnp.zeros((TILE, width), jnp.float32)
    after = jnp.zeros((TILE, width), jnp.float32)
    for entry, (_, _, _, (on_0, on_1), _) in enumerate(entries):
        if any(o & (o + 1) == 0 and o for o in (on_0, on_1)):
            offset = jnp.where(first, on_0, on_1)
            candidate = source_rows(entry)
            before = jnp.where(jnp.bitwise_xor(here, here - 1) == offset, candidate, before)
            after = jnp.where(jnp.bitwise_xor(here, here + 1) == offset, candidate, after)
    row_group = lax.broadcasted_iota(jnp.int32, (groups, width), 0)
    own_group = row_group == lax.broadcasted_iota(jnp.int32, (groups, width), 1) // channels
    spread = []
    for part in (before, source_rows(0), after):
        for h in range(window):
            line = jnp.broadcast_to(part[h : h + 1, :], (groups, width))
            spread.append(jnp.where(own_group, line, 0.0))
    spread += [jnp.zeros((groups, width), jnp.float32)] * (planes_padded(planes, count) - planes)
    spread = jnp.concatenate(spread, axis=0).astype(jnp.bfloat16)
    spread_ref[...] = spread

    base, edge = [], []
    for entry in range(count):
        mine, other = near[entry], far[entry]
        if entries[entry][4] % 2:
            mine, other = other, mine
        base.append(mine[:rows, :])
        edge.append(block.beside(other))
    base = correlate(jnp.concatenate(base, axis=0), spread, channels).astype(base_ref.dtype)
    edge = jnp.concatenate(edge, axis=0).astype(jnp.bfloat16)
    edge = block.keep_inside(correlate(edge, spread, channels))
    base_ref[...] = jnp.concatenate(planes_of(base, count, planes, groups), axis=0)
    edge_ref[...] = jnp.concatenate(planes_of(edge, count, planes, groups), axis=0)


def with_column(stacked, product, column, planes, groups):
    rows = product.shape[0]
    short = -product.shape[1] % LANES
    if short:
        product = jnp.concatenate([product, jnp.zeros((rows, short), product.dtype)], axis=1)
    here = lax.broadcasted_iota(jnp.int32, (rows, LANES), 1) // groups == column
    result = []
    for plane in range(planes):
        tile, place = divmod(plane * groups, LANES)
        piece = product[:, tile * LANES : (tile + 1) * LANES]
        shift = (column * groups - place) % LANES
        piece = pltpu.roll(piece, shift, 1) if shift else piece
        result.append(jnp.where(here, piece, stacked[plane]))
    return result


def filter_kernel(entries, groups, window, base_ref, edge_ref, spread_ref, last_ref, *refs):
    band_one, blocks, band_two, out_ref = refs
    rows = out_ref.shape[1]
    high = rows + TILE
    planes = 3 * window
    channels = spread_ref.shape[1] // groups
    block = Block(rows)
    spread = spread_ref[...]
    last = max(part for part, _, _, _, _ in entries)
    base = [base_ref[plane * rows : (plane + 1) * rows, :] for plane in range(planes)]
    edge = [edge_ref[plane * TILE : (plane + 1) * TILE, :] for plane in range(planes)]
    for column, (part, _, k, _, hops) in enumerate(entries):
        if part != last:
            continue
        brought = last_ref.at[k]
        if hops % 2:
            product = correlate(brought[:rows, :], spread, channels).astype(base_ref.dtype)
            base = with_column(base, product, column, planes, groups)
        else:
            product = correlate(block.beside(brought).astype(jnp.bfloat16), spread, channels)
            edge = with_column(edge, block.keep_inside(product), column, planes, groups)
    base = jnp.concatenate(base, axis=0)
    edge = jnp.concatenate(edge, axis=0).astype(jnp.bfloat16)

    base = jnp.dot(base, band_one[...], preferred_element_type=jnp.float32)
    edge = jnp.dot(edge, band_one[...], preferred_element_type=jnp.float32)
    one = []
    for plane in range(planes):
        product = jnp.concatenate(
            [base[plane * rows : (plane + 1) * rows], edge[plane * TILE : (plane + 1) * TILE]],
            axis=0,
        )
        total = jnp.maximum(shifted_sum(product), 0.0)
        one += [total[:rows], block.keep_inside(total[rows:])]
    one = jnp.concatenate(one, axis=0).astype(jnp.bfloat16).reshape(3, window * high, LANES)
    product = jnp.dot(
        jnp.concatenate([one[0], one[1], one[2]], axis=1),
        blocks[...],
        preferred_element_type=jnp.float32,
    )
    product = product.reshape(window, high, 3 * LANES)
    two = []
    for h in range(window):
        total = product[h, :, LANES : 2 * LANES]
        if h > 0:
            total = total + product[h - 1, :, :LANES]
        if h < window - 1:
            total = total + product[h + 1, :, 2 * LANES :]
        two.append(jnp.maximum(total, 0.0))
    taps = jnp.concatenate([row_taps(plane) for plane in two], axis=0).astype(jnp.bfloat16)
    three = jnp.dot(taps, band_two[...], preferred_element_type=jnp.float32)
    three = three.reshape(window, high, LANES)[:, :rows]
    out_ref[...] = jnp.maximum(three, 0.0).astype(out_ref.dtype)


def local_call(kernel, out_shape, *operands):
    vmem = pl.BlockSpec(memory_space=pltpu.VMEM)
    return pl.pallas_call(
        kernel,
        out_shape=out_shape,
        in_specs=[vmem] * len(operands),
        out_specs=jax.tree.map(lambda _: vmem, out_shape),
        compiler_params=pltpu.CompilerParams(vmem_limit_bytes=8 << 20),
    )(*operands)


def filter_all(near, far, matrices, entries, groups, window, rows):
    *far, last = far
    planes = 3 * window
    width = near[0].shape[2]
    volume = local_call(
        functools.partial(volume_kernel, entries, groups, window),
        [
            jax.ShapeDtypeStruct((planes * rows, LANES), jnp.bfloat16),
            jax.ShapeDtypeStruct((planes * TILE, LANES), jnp.float32),
            jax.ShapeDtypeStruct(
                (planes_padded(planes, LANES // groups) * groups, width), jnp.bfloat16
            ),
        ],
        *near,
        *far,
    )
    return local_call(
        functools.partial(filter_kernel, entries, groups, window),
        jax.ShapeDtypeStruct((window, rows, LANES), jnp.bfloat16),
        *volume,
        last,
        *matrices,
    )


def fast_local(
    source_features,
    target_features,
    source_rows,
    target_cols,
    target_kernel_one,
    source_kernel,
    target_kernel_two,
):
    groups = source_kernel.shape[2]
    window = source_rows.shape[0]
    rows = target_features.shape[0]
    count = lax.axis_size("src")
    entries = entries_of(count)
    height = rows + -(-window // TILE) * TILE

    def exchange(block, mask):
        pairs = [(2 * s + t, 2 * (s ^ mask[t]) + 1 - t) for s in range(count) for t in range(2)]
        return lax.ppermute(block, ("src", "tgt"), pairs)

    held, kernels = pack(
        source_rows,
        source_features[:, 0],
        target_features[:, 0],
        (target_cols, target_kernel_one, source_kernel, target_kernel_two),
        height,
    )
    *early, last = rounds_of(count)
    matrices = None
    for ((mask, _),) in early:
        arrived = exchange(held, (mask, mask))
        if matrices is None:
            matrices = weights(*kernels, [offsets for _, _, _, offsets, _ in entries])
            arrived, matrices = lax.optimization_barrier((arrived, matrices))
        held = jnp.concatenate([held, arrived], axis=0)
    if matrices is None:
        matrices = weights(*kernels, [offsets for _, _, _, offsets, _ in entries])
    near = [held, *(exchange(held, mask) for mask in last)]
    far = [exchange(part, (0, 0)) for part in near]
    return filter_all(near, far, matrices, entries, groups, window, rows)[:, None]


def with_halo(block, sides, width):
    for axis, dim in sides:
        count = lax.axis_size(axis)
        forward = [(i, i + 1) for i in range(count - 1)]
        backward = [(target, source) for source, target in forward]
        low = lax.ppermute(
            lax.slice_in_dim(block, block.shape[dim] - width, None, axis=dim), axis, forward
        )
        high = lax.ppermute(lax.slice_in_dim(block, 0, width, axis=dim), axis, backward)
        block = jnp.concatenate([low, block, high], axis=dim)
    return block


def build_toeplitz(kernel, breadth):
    groups = kernel.shape[2]
    span_width = breadth * groups
    row_index = lax.broadcasted_iota(jnp.int32, (3, breadth, breadth), 1)
    col_index = lax.broadcasted_iota(jnp.int32, (3, breadth, breadth), 2)
    tap_index = lax.broadcasted_iota(jnp.int32, (3, breadth, breadth), 0)
    shifts = (row_index - col_index == tap_index - 1).astype(jnp.bfloat16)
    matrices = []
    for offset_y in range(3):
        banded = jnp.einsum(
            "xab,xio->aibo", shifts, kernel[offset_y], preferred_element_type=jnp.float32
        )
        matrices.append(banded.astype(jnp.bfloat16).reshape(span_width, span_width))
    return jnp.stack(matrices)


def banded_pass(slices, matrices):
    span_width = matrices.shape[1]
    running = jnp.dot(
        slices[0].reshape(-1, span_width), matrices[0], preferred_element_type=jnp.float32
    )
    for offset in range(1, 3):
        running = running + jnp.dot(
            slices[offset].reshape(-1, span_width),
            matrices[offset],
            preferred_element_type=jnp.float32,
        )
    return jnp.maximum(running, 0.0).astype(jnp.bfloat16).reshape(slices[0].shape)


def target_pass(padded, matrices):
    row_count = padded.shape[1] - 2
    return banded_pass([padded[:, offset : offset + row_count] for offset in range(3)], matrices)


def column_filter(neighbours, source_kernel, groups, window_rows):
    bordered = jnp.pad(neighbours, ((0, 0), (1, 1), (0, 0), (0, 0)))
    span_width = neighbours.shape[3]
    repeats = math.gcd(span_width // groups, max(1, 128 // groups))
    block_width = repeats * groups
    diagonal = jnp.einsum(
        "ab,yxij->yxaibj", jnp.eye(repeats, dtype=jnp.float32), source_kernel.astype(jnp.float32)
    )
    diagonal = diagonal.reshape(3, 3, block_width, block_width).astype(jnp.bfloat16)
    running = jnp.zeros((neighbours[1].size // block_width, block_width), jnp.float32)
    for offset in range(3):
        window = bordered[:, offset : offset + window_rows].reshape(3, -1, block_width)
        running = running + jnp.einsum(
            "xmc,xcd->md", window, diagonal[offset], preferred_element_type=jnp.float32
        )
    return jnp.maximum(running, 0.0).astype(jnp.bfloat16).reshape(neighbours[1].shape)


def local(
    source_features,
    target_features,
    source_rows,
    target_cols,
    target_kernel_one,
    source_kernel,
    target_kernel_two,
):
    groups = source_kernel.shape[2]
    channels = source_features.shape[2] // groups
    window_rows = source_rows.shape[0]
    selected = jnp.take(source_features[:, 0], source_rows, axis=0)
    columns = selected[None]
    column_count = columns.shape[0]
    columns = columns.reshape(column_count, window_rows, groups, channels)
    gathered = lax.all_gather(target_features, "src", axis=1, tiled=True)
    gathered = jnp.take(gathered, target_cols, axis=1)
    target_rows = gathered.shape[0]
    breadth = gathered.shape[1]
    grouped = gathered.reshape(target_rows, breadth, groups, channels)
    volume = jnp.einsum("khgc,rwgc->khrwg", columns, grouped, preferred_element_type=jnp.float32)
    volume = (
        (volume * channels ** (-0.5))
        .astype(jnp.bfloat16)
        .reshape(column_count * window_rows, target_rows, breadth * groups)
    )
    padded = with_halo(volume, (("tgt", 1),), 1)
    filtered_one = target_pass(padded, build_toeplitz(target_kernel_one, breadth))
    neighbours = with_halo(filtered_one[None], (("src", 0),), 1)
    filtered_two = column_filter(neighbours, source_kernel, groups, window_rows)
    padded_last = with_halo(filtered_two, (("tgt", 1),), 1)
    filtered_three = target_pass(padded_last, build_toeplitz(target_kernel_two, breadth))
    return filtered_three[:, None]


def solution(mesh):
    def step(*args):
        source, target, source_rows, cols, _, source_kernel, _ = args
        count = lax.axis_size("src")
        fits = (
            lax.axis_size("tgt") == 2
            and count > 1
            and count & (count - 1) == 0
            and source.shape[1] == 1
            and target.shape[1] == 1
            and cols.shape[0] == count
            and count * source_kernel.shape[2] == LANES
            and source_rows.shape[0] <= TILE
            and target.shape[0] % (2 * TILE) == 0
        )
        return (fast_local if fits else local)(*args)

    return jax.shard_map(
        step,
        mesh=mesh,
        in_specs=(
            P("pair", "src", None),
            P(("pair", "tgt"), "src", None),
            P("pair"),
            P("pair"),
            P(),
            P(),
            P(),
        ),
        out_specs=P("pair", "src", "tgt", None),
        check_vma=False,
    )
```

profile of v0, /device:TPU:0, one launch (start us, length us, event | category | flops | bytes accessed | tf_op | source)
XLA Modules:
  0.0 15.4 jit_solution(10377873470056732347)
XLA Ops:
  0.0 0.9 %pack.1 = (bf16[1,40,256]{2,1,0:T(8,128)(2,1)S(1)}, s32[8]{0:T(128)S(1)}, bf16[3,3,16,16]{3,2,1,0:T(8,128)(2,1)S(1)}, bf16[3,3,16,16]{3,2,1,0:T(8,128)(2,1)S(1)}, bf16[3,3,16,16]{3,2,1,0:T(8,128)(2,1)S(1)}) custom-call(s32[4]{0:T(128)} %rows_hbm.1, bf16[32,256]{1,0:T(8,128)(2,1)} %bitcast.5, bf16[32,256]{1,0:T(8,128)(2,1)} %bitcast.6, s32[8]{0:T(128)} %refs_0_.1, ...), custom_call_target="tpu_custom_call" | custom-call | tf_op jit(solution)/shard_map/pack/pallas_call | solution.py:75
  0.9 3.6 %collective-permute-start = (bf16[1,40,256]{2,1,0:T(8,128)(2,1)S(1)}, bf16[1,40,256]{2,1,0:T(8,128)(2,1)S(1)}, u32[]{:S(2)}, u32[]{:S(2)}) collective-permute-start(bf16[1,40,256]{2,1,0:T(8,128)(2,1)S(1)} %get-tuple-element.20), channel_id=1, source_target_pairs={{0,9},{1,8},{2,11},{3,10},{4,13},{5,12},{6,15},{7,14},{8,1},{9,0},... | collective-permute-start | bytes 61448 | tf_op jit(solution)/shard_map/ppermute | solution.py:415
  4.5 0.8 %weights.1 = (bf16[128,384]{1,0:T(8,128)(2,1)S(1)}, bf16[384,384]{1,0:T(8,128)(2,1)S(1)}, bf16[384,128]{1,0:T(8,128)(2,1)S(1)}) custom-call(s32[8]{0:T(128)S(1)} %get-tuple-element.21.cols_ref, bf16[3,3,16,16]{3,2,1,0:T(8,128)(2,1)S(1)} %get-tuple-element.22.one_ref, bf16[3,3,16,16]{3,2,1,0:T(8,128)(2,1)S(1)} %get-tuple-element.23.source_ref, ...), custom_call_target="tpu_custom_call" | custom-call | tf_op jit(solution)/shard_map/weights/pallas_call | solution.py:146
  5.3 0.7 %collective-permute-done = bf16[1,40,256]{2,1,0:T(8,128)(2,1)S(1)} collective-permute-done((bf16[1,40,256]{2,1,0:T(8,128)(2,1)S(1)}, bf16[1,40,256]{2,1,0:T(8,128)(2,1)S(1)}, u32[]{:S(2)}, u32[]{:S(2)}) %collective-permute-start) | collective-permute-done | bytes 20512 | tf_op jit(solution)/shard_map/ppermute | solution.py:415
  6.0 1.8 %collective-permute-start.1 = (bf16[2,40,256]{2,1,0:T(8,128)(2,1)S(1)}, bf16[2,40,256]{2,1,0:T(8,128)(2,1)S(1)}, u32[]{:S(2)}, u32[]{:S(2)}) collective-permute-start(bf16[2,40,256]{2,1,0:T(8,128)(2,1)S(1)} %constant_dynamic-update-slice_fusion.refs_0_), channel_id=1, source_target_pairs={{0,3},{1,4},{2,1},{3,6},{4,7},{5,0},{6,5},{7,2},{8,11},{9,12},{10,... | collective-permute-start | bytes 122888 | tf_op jit(solution)/shard_map/ppermute | solution.py:415
  7.8 0.1 collective-permute-start.2
  7.9 2.7 %collective-permute-start.3 = (bf16[2,40,256]{2,1,0:T(8,128)(2,1)S(1)}, bf16[2,40,256]{2,1,0:T(8,128)(2,1)S(1)}, u32[]{:S(2)}, u32[]{:S(2)}) collective-permute-start(bf16[2,40,256]{2,1,0:T(8,128)(2,1)S(1)} %constant_dynamic-update-slice_fusion.refs_0_), channel_id=1, source_target_pairs={{0,7},{1,6},{2,5},{3,4},{4,3},{5,2},{6,1},{7,0},{8,15},{9,14},{10,... | collective-permute-start | bytes 122888 | tf_op jit(solution)/shard_map/ppermute | solution.py:415
  10.5 0.4 %collective-permute-start.4 = (bf16[2,40,256]{2,1,0:T(8,128)(2,1)S(1)}, bf16[2,40,256]{2,1,0:T(8,128)(2,1)S(1)}, u32[]{:S(2)}, u32[]{:S(2)}) collective-permute-start(bf16[2,40,256]{2,1,0:T(8,128)(2,1)S(1)} %constant_dynamic-update-slice_fusion.refs_0_), channel_id=1, source_target_pairs={{0,1},{1,0},{2,3},{3,2},{4,5},{5,4},{6,7},{7,6},{8,9},{9,8},{10,11... | collective-permute-start | bytes 122888 | tf_op jit(solution)/shard_map/ppermute | solution.py:415
  10.9 0.0 collective-permute-done.1.refs_1_
  10.9 0.1 collective-permute-start.5
  11.1 0.2 collective-permute-done.2.refs_2_
  11.2 0.8 %collective-permute-start.6 = (bf16[2,40,256]{2,1,0:T(8,128)(2,1)S(1)}, bf16[2,40,256]{2,1,0:T(8,128)(2,1)S(1)}, u32[]{:S(2)}, u32[]{:S(2)}) collective-permute-start(bf16[2,40,256]{2,1,0:T(8,128)(2,1)S(1)} %collective-permute-done.2.refs_2_), channel_id=1, source_target_pairs={{0,1},{1,0},{2,3},{3,2},{4,5},{5,4},{6,7},{7,6},{8,9},{9,8},{10,11... | collective-permute-start | bytes 122888 | tf_op jit(solution)/shard_map/ppermute | solution.py:415
  12.0 0.2 %collective-permute-done.3.refs_3_ = bf16[2,40,256]{2,1,0:T(8,128)(2,1)S(1)} collective-permute-done((bf16[2,40,256]{2,1,0:T(8,128)(2,1)S(1)}, bf16[2,40,256]{2,1,0:T(8,128)(2,1)S(1)}, u32[]{:S(2)}, u32[]{:S(2)}) %collective-permute-start.3) | collective-permute-done | bytes 40992 | tf_op jit(solution)/shard_map/ppermute | solution.py:415
  12.2 0.8 %collective-permute-start.7 = (bf16[2,40,256]{2,1,0:T(8,128)(2,1)S(1)}, bf16[2,40,256]{2,1,0:T(8,128)(2,1)S(1)}, u32[]{:S(2)}, u32[]{:S(2)}) collective-permute-start(bf16[2,40,256]{2,1,0:T(8,128)(2,1)S(1)} %collective-permute-done.3.refs_3_), channel_id=1, source_target_pairs={{0,1},{1,0},{2,3},{3,2},{4,5},{5,4},{6,7},{7,6},{8,9},{9,8},{10,11... | collective-permute-start | bytes 122888 | tf_op jit(solution)/shard_map/ppermute | solution.py:415
  13.1 0.0 collective-permute-done.4.refs_4_
  13.1 0.0 collective-permute-done.5.refs_5_
  13.1 0.0 collective-permute-done.6.refs_6_
  13.1 0.5 %shard_map.73 = (bf16[384,128]{1,0:T(8,128)(2,1)S(1)}, f32[96,128]{1,0:T(8,128)S(1)}, bf16[192,256]{1,0:T(8,128)(2,1)S(1)}) custom-call(bf16[2,40,256]{2,1,0:T(8,128)(2,1)S(1)} %constant_dynamic-update-slice_fusion.refs_0_, bf16[2,40,256]{2,1,0:T(8,128)(2,1)S(1)} %collective-permute-done.1.refs_1_, bf16[2,40,256]{2,1,0:T(8,128)(2,1)S(1)} %collective-permute-done.2.refs_2_, ...), custom_call_target="tpu_custom_call" | custom-call | tf_op jit(solution)/shard_map/pallas_call | solution.py:363
  13.5 0.4 %collective-permute-done.7.last_ref = bf16[2,40,256]{2,1,0:T(8,128)(2,1)S(1)} collective-permute-done((bf16[2,40,256]{2,1,0:T(8,128)(2,1)S(1)}, bf16[2,40,256]{2,1,0:T(8,128)(2,1)S(1)}, u32[]{:S(2)}, u32[]{:S(2)}) %collective-permute-start.7) | collective-permute-done | bytes 40992 | tf_op jit(solution)/shard_map/ppermute | solution.py:415
  13.9 1.4 %shard_map.74 = bf16[4,32,128]{2,1,0:T(8,128)(2,1)} custom-call(bf16[384,128]{1,0:T(8,128)(2,1)S(1)} %get-tuple-element.29.base_ref, f32[96,128]{1,0:T(8,128)S(1)} %get-tuple-element.30.edge_ref, bf16[192,256]{1,0:T(8,128)(2,1)S(1)} %get-tuple-element.31.spread_ref, bf16[2,40,256]{2,1,0:T(8,128)(2,1)S(1)} %collective-permute-done.7.last_ref, ...), custom_call_target="tpu_custom_call" | custom-call | tf_op jit(solution)/shard_map/pallas_call | solution.py:363
  (2 shorter events, 0.0 us)
Async XLA Ops:
  0.9 5.1 %collective-permute-start = (bf16[1,40,256]{2,1,0:T(8,128)(2,1)S(1)}, bf16[1,40,256]{2,1,0:T(8,128)(2,1)S(1)}, u32[]{:S(2)}, u32[]{:S(2)}) collective-permute-start(bf16[1,40,256]{2,1,0:T(8,128)(2,1)S(1)} %get-tuple-element.20), channel_id=1, source_target_pairs={{0,9},{1,8},{2,11},{3,10},{4,13},{5,12},{6,15},{7,14},{8,1},{9,0},... | collective-permute-start | bytes 61448 | tf_op jit(solution)/shard_map/ppermute | solution.py:415
  6.0 4.9 %collective-permute-start.1 = (bf16[2,40,256]{2,1,0:T(8,128)(2,1)S(1)}, bf16[2,40,256]{2,1,0:T(8,128)(2,1)S(1)}, u32[]{:S(2)}, u32[]{:S(2)}) collective-permute-start(bf16[2,40,256]{2,1,0:T(8,128)(2,1)S(1)} %constant_dynamic-update-slice_fusion.refs_0_), channel_id=1, source_target_pairs={{0,3},{1,4},{2,1},{3,6},{4,7},{5,0},{6,5},{7,2},{8,11},{9,12},{10,... | collective-permute-start | bytes 122888 | tf_op jit(solution)/shard_map/ppermute | solution.py:415
  7.8 3.4 %collective-permute-start.2 = (bf16[2,40,256]{2,1,0:T(8,128)(2,1)S(1)}, bf16[2,40,256]{2,1,0:T(8,128)(2,1)S(1)}, u32[]{:S(2)}, u32[]{:S(2)}) collective-permute-start(bf16[2,40,256]{2,1,0:T(8,128)(2,1)S(1)} %constant_dynamic-update-slice_fusion.refs_0_), channel_id=1, source_target_pairs={{0,5},{1,2},{2,7},{3,0},{4,1},{5,6},{6,3},{7,4},{8,13},{9,10},{10,... | collective-permute-start | bytes 122888 | tf_op jit(solution)/shard_map/ppermute | solution.py:415
  7.9 4.4 %collective-permute-start.3 = (bf16[2,40,256]{2,1,0:T(8,128)(2,1)S(1)}, bf16[2,40,256]{2,1,0:T(8,128)(2,1)S(1)}, u32[]{:S(2)}, u32[]{:S(2)}) collective-permute-start(bf16[2,40,256]{2,1,0:T(8,128)(2,1)S(1)} %constant_dynamic-update-slice_fusion.refs_0_), channel_id=1, source_target_pairs={{0,7},{1,6},{2,5},{3,4},{4,3},{5,2},{6,1},{7,0},{8,15},{9,14},{10,... | collective-permute-start | bytes 122888 | tf_op jit(solution)/shard_map/ppermute | solution.py:415
  10.5 2.5 %collective-permute-start.4 = (bf16[2,40,256]{2,1,0:T(8,128)(2,1)S(1)}, bf16[2,40,256]{2,1,0:T(8,128)(2,1)S(1)}, u32[]{:S(2)}, u32[]{:S(2)}) collective-permute-start(bf16[2,40,256]{2,1,0:T(8,128)(2,1)S(1)} %constant_dynamic-update-slice_fusion.refs_0_), channel_id=1, source_target_pairs={{0,1},{1,0},{2,3},{3,2},{4,5},{5,4},{6,7},{7,6},{8,9},{9,8},{10,11... | collective-permute-start | bytes 122888 | tf_op jit(solution)/shard_map/ppermute | solution.py:415
  10.9 2.1 %collective-permute-start.5 = (bf16[2,40,256]{2,1,0:T(8,128)(2,1)S(1)}, bf16[2,40,256]{2,1,0:T(8,128)(2,1)S(1)}, u32[]{:S(2)}, u32[]{:S(2)}) collective-permute-start(bf16[2,40,256]{2,1,0:T(8,128)(2,1)S(1)} %collective-permute-done.1.refs_1_), channel_id=1, source_target_pairs={{0,1},{1,0},{2,3},{3,2},{4,5},{5,4},{6,7},{7,6},{8,9},{9,8},{10,11... | collective-permute-start | bytes 122888 | tf_op jit(solution)/shard_map/ppermute | solution.py:415
  11.2 1.9 %collective-permute-start.6 = (bf16[2,40,256]{2,1,0:T(8,128)(2,1)S(1)}, bf16[2,40,256]{2,1,0:T(8,128)(2,1)S(1)}, u32[]{:S(2)}, u32[]{:S(2)}) collective-permute-start(bf16[2,40,256]{2,1,0:T(8,128)(2,1)S(1)} %collective-permute-done.2.refs_2_), channel_id=1, source_target_pairs={{0,1},{1,0},{2,3},{3,2},{4,5},{5,4},{6,7},{7,6},{8,9},{9,8},{10,11... | collective-permute-start | bytes 122888 | tf_op jit(solution)/shard_map/ppermute | solution.py:415
  12.2 1.7 %collective-permute-start.7 = (bf16[2,40,256]{2,1,0:T(8,128)(2,1)S(1)}, bf16[2,40,256]{2,1,0:T(8,128)(2,1)S(1)}, u32[]{:S(2)}, u32[]{:S(2)}) collective-permute-start(bf16[2,40,256]{2,1,0:T(8,128)(2,1)S(1)} %collective-permute-done.3.refs_3_), channel_id=1, source_target_pairs={{0,1},{1,0},{2,3},{3,2},{4,5},{5,4},{6,7},{7,6},{8,9},{9,8},{10,11... | collective-permute-start | bytes 122888 | tf_op jit(solution)/shard_map/ppermute | solution.py:415
where the time goes:
time: 15.5 us; the launch traced here: 15.4 us
  starting transfers between devices  10.2 us (66%)
  Pallas kernels  3.61 us (23%)
  waiting for transfers between devices  1.49 us (10%)
    ppermute x8, starting transfers between devices, exchange(): return lax.ppermute(block, ('src', 'tgt'), pairs)  10.2 us
    pallas_call x2, Pallas kernels, local_call(): pl.pallas_call(kernel, out_shape=out_shape, in_specs=[vmem] * len(operand...  1.89 us
    ppermute x8, waiting for transfers between devices, exchange(): return lax.ppermute(block, ('src', 'tgt'), pairs)  1.49 us
    pallas_call x1, Pallas kernels, pack(): pl.pallas_call(functools.partial(pack_kernel, len(kernels)), out_shape=[j...  0.91 us
    pallas_call x1, Pallas kernels, weights(): pl.pallas_call(functools.partial(weights_kernel, offsets), out_shape=[jax...  0.8 us
  transfers between devices with their start and end apart: 8, of which 4 were waited for; matrix products, arithmetic and copies ran while one was open for 0% of the time, Pallas kernels for 8%

commit v1 on v0

--- a/solution.py
+++ b/solution.py
@@ -11,6 +11,10 @@
 
 LANES = 128
 TILE = 8
+
+
+def whole_tiles(rows):
+    return -(-rows // TILE) * TILE
 
 
 def rounds_of(count):
@@ -37,59 +41,61 @@
     return entries
 
 
-def pack_kernel(count, rows_hbm, source_hbm, target_hbm, *refs):
-    kernels, (out_ref, *held), (rows_ref, source_ref, wide_ref, sems) = (
-        refs[:count],
-        refs[count : 2 * count + 1],
-        refs[2 * count + 1 :],
-    )
-    rows = target_hbm.shape[0]
-    window = rows_hbm.shape[0]
+def fetch(pairs, sems):
     copies = [
         pltpu.make_async_copy(source, target, sems.at[index])
-        for index, (source, target) in enumerate(
-            [
-                (rows_hbm, rows_ref),
-                (source_hbm, source_ref),
-                (target_hbm, out_ref.at[0, pl.ds(0, rows)]),
-                *zip(kernels, held, strict=True),
-            ]
-        )
+        for index, (source, target) in enumerate(pairs)
     ]
     for copy in copies:
         copy.start()
+    return copies
+
+
+def pack_kernel(rows_hbm, source_hbm, target_hbm, out_ref, rows_ref, source_ref, wide_ref, sems):
+    rows = target_hbm.shape[0]
+    window = rows_hbm.shape[0]
+    copies = fetch(
+        [
+            (rows_hbm, rows_ref),
+            (source_hbm, source_ref),
+            (target_hbm, out_ref.at[pl.ds(0, rows)]),
+        ],
+        sems,
+    )
     copies[1].wait()
     wide_ref[...] = source_ref[...].astype(jnp.float32)
     copies[0].wait()
     lines = [wide_ref[pl.ds(rows_ref[h], 1), :] for h in range(window)]
-    blank = out_ref.shape[1] - rows - window
+    blank = out_ref.shape[0] - rows - window
     if blank:
         lines.append(jnp.zeros((blank, wide_ref.shape[1]), jnp.float32))
-    out_ref[0, rows:, :] = jnp.concatenate(lines, axis=0).astype(out_ref.dtype)
-    for copy in copies[2:]:
-        copy.wait()
-
-
-def pack(source_rows, source, target, kernels, height):
-    operands = (source_rows, source, target, *kernels)
-    out, *held = pl.pallas_call(
-        functools.partial(pack_kernel, len(kernels)),
-        out_shape=[
-            jax.ShapeDtypeStruct((1, height, target.shape[1]), target.dtype),
-            *(jax.ShapeDtypeStruct(kernel.shape, kernel.dtype) for kernel in kernels),
-        ],
+    out_ref[rows:, :] = jnp.concatenate(lines, axis=0).astype(out_ref.dtype)
+    copies[2].wait()
+
+
+def from_hbm(kernel, out_shape, operands, scratch):
+    return pl.pallas_call(
+        kernel,
+        out_shape=out_shape,
         in_specs=[pl.BlockSpec(memory_space=pltpu.HBM)] * len(operands),
-        out_specs=[pl.BlockSpec(memory_space=pltpu.VMEM)] * (1 + len(kernels)),
-        scratch_shapes=[
+        out_specs=jax.tree.map(lambda _: pl.BlockSpec(memory_space=pltpu.VMEM), out_shape),
+        scratch_shapes=[*scratch, pltpu.SemaphoreType.DMA((len(operands),))],
+        compiler_params=pltpu.CompilerParams(vmem_limit_bytes=4 << 20),
+    )(*(pltpu.with_memory_space_constraint(x, pltpu.HBM) for x in operands))
+
+
+def pack(source_rows, source, target):
+    height = target.shape[0] + whole_tiles(source_rows.shape[0])
+    return from_hbm(
+        pack_kernel,
+        jax.ShapeDtypeStruct((height, target.shape[1]), target.dtype),
+        (source_rows, source, target),
+        [
             pltpu.SMEM(source_rows.shape, source_rows.dtype),
             pltpu.VMEM(source.shape, source.dtype),
             pltpu.VMEM(source.shape, jnp.float32),
-            pltpu.SemaphoreType.DMA((3 + len(kernels),)),
         ],
-        compiler_params=pltpu.CompilerParams(vmem_limit_bytes=4 << 20),
-        name="pack",
-    )(*(pltpu.with_memory_space_constraint(x, pltpu.HBM) for x in operands))
-    return out, held
+    )
 
 
 def widen(block):
@@ -113,7 +119,11 @@
     return total
 
 
-def weights_kernel(offsets, cols_ref, one_ref, source_ref, two_ref, band_one, blocks, band_two):
+def weights_kernel(offsets, *refs):
+    operands, (band_one, blocks, band_two), (*scratch, sems) = refs[:4], refs[4:7], refs[7:]
+    cols_ref, one_ref, source_ref, two_ref = scratch
+    for copy in fetch(zip(operands, scratch, strict=True), sems):
+        copy.wait()
     groups = one_ref.shape[2]
     breadth = LANES // groups
     here = lax.axis_index("src")
@@ -140,21 +150,21 @@
                 blocks[row : row + groups, lanes] = piece.astype(blocks.dtype)
 
 
-def weights(target_cols, one, source, two, offsets):
-    smem = pl.BlockSpec(memory_space=pltpu.SMEM)
-    vmem = pl.BlockSpec(memory_space=pltpu.VMEM)
-    return pl.pallas_call(
+def weights(target_cols, kernels, offsets):
+    dtype = kernels[0].dtype
+    return from_hbm(
         functools.partial(weights_kernel, offsets),
-        out_shape=[
-            jax.ShapeDtypeStruct((LANES, 3 * LANES), one.dtype),
-            jax.ShapeDtypeStruct((3 * LANES, 3 * LANES), one.dtype),
-            jax.ShapeDtypeStruct((3 * LANES, LANES), one.dtype),
+        [
+            jax.ShapeDtypeStruct((LANES, 3 * LANES), dtype),
+            jax.ShapeDtypeStruct((3 * LANES, 3 * LANES), dtype),
+            jax.ShapeDtypeStruct((3 * LANES, LANES), dtype),
         ],
-        in_specs=[smem, vmem, vmem, vmem],
-        out_specs=[vmem, vmem, vmem],
-        compiler_params=pltpu.CompilerParams(vmem_limit_bytes=4 << 20),
-        name="weights",
-    )(target_cols, one, source, two)
+        (target_cols, *kernels),
+        [
+            pltpu.SMEM(target_cols.shape, target_cols.dtype),
+            *(pltpu.VMEM(kernel.shape, kernel.dtype) for kernel in kernels),
+        ],
+    )
 
 
 def shifted_sum(product):
@@ -237,7 +247,7 @@
 def volume_kernel(entries, groups, window, *refs):
     *parts, base_ref, edge_ref, spread_ref = refs
     count = len(entries)
-    width = parts[0].shape[2]
+    width = parts[0].shape[1]
     planes = 3 * window
     rows = base_ref.shape[0] // planes
     channels = width // groups
@@ -245,17 +255,20 @@
     block = Block(rows)
     first = block.first
     half = (len(parts) + 1) // 2
-    near = [parts[part].at[k] for part, _, k, _, _ in entries]
+    held = 1 + max(k for _, _, k, _, _ in entries)
+    near = [parts[part].at[pl.ds(k * rows, rows)] for part, _, k, _, _ in entries]
     far = [
-        parts[half + twin].at[k] if half + twin < len(parts) else parts[part].at[k]
+        parts[half + twin if half + twin < len(parts) else part].at[pl.ds(k * rows, rows)]
         for part, twin, k, _, _ in entries
     ]
 
     def source_rows(entry):
-        return near[entry][rows : rows + TILE, :].astype(jnp.float32)
-
-    before = jnp.zeros((TILE, width), jnp.float32)
-    after = jnp.zeros((TILE, width), jnp.float32)
+        part, _, k, _, _ = entries[entry]
+        lines = parts[part][held * rows :, :].astype(jnp.float32)
+        return lines[k * window : (k + 1) * window]
+
+    before = jnp.zeros((window, width), jnp.float32)
+    after = jnp.zeros((window, width), jnp.float32)
     for entry, (_, _, _, (on_0, on_1), _) in enumerate(entries):
         if any(o & (o + 1) == 0 and o for o in (on_0, on_1)):
             offset = jnp.where(first, on_0, on_1)
@@ -317,7 +330,7 @@
     for column, (part, _, k, _, hops) in enumerate(entries):
         if part != last:
             continue
-        brought = last_ref.at[k]
+        brought = last_ref.at[pl.ds(k * rows, rows)]
         if hops % 2:
             product = correlate(brought[:rows, :], spread, channels).astype(base_ref.dtype)
             base = with_column(base, product, column, planes, groups)
@@ -372,7 +385,7 @@
 def filter_all(near, far, matrices, entries, groups, window, rows):
     *far, last = far
     planes = 3 * window
-    width = near[0].shape[2]
+    width = near[0].shape[1]
     volume = local_call(
         functools.partial(volume_kernel, entries, groups, window),
         [
@@ -408,29 +421,24 @@
     rows = target_features.shape[0]
     count = lax.axis_size("src")
     entries = entries_of(count)
-    height = rows + -(-window // TILE) * TILE
 
     def exchange(block, mask):
         pairs = [(2 * s + t, 2 * (s ^ mask[t]) + 1 - t) for s in range(count) for t in range(2)]
         return lax.ppermute(block, ("src", "tgt"), pairs)
 
-    held, kernels = pack(
-        source_rows,
-        source_features[:, 0],
-        target_features[:, 0],
-        (target_cols, target_kernel_one, source_kernel, target_kernel_two),
-        height,
-    )
-    *early, last = rounds_of(count)
-    matrices = None
-    for ((mask, _),) in early:
-        arrived = exchange(held, (mask, mask))
-        if matrices is None:
-            matrices = weights(*kernels, [offsets for _, _, _, offsets, _ in entries])
-            arrived, matrices = lax.optimization_barrier((arrived, matrices))
-        held = jnp.concatenate([held, arrived], axis=0)
-    if matrices is None:
-        matrices = weights(*kernels, [offsets for _, _, _, offsets, _ in entries])
+    early, last = rounds_of(count)
+    ((mask, _),) = early
+    held = pack(source_rows, source_features[:, 0], target_features[:, 0])
+    arrived = exchange(held, (mask, mask))
+    matrices = weights(
+        target_cols,
+        (target_kernel_one, source_kernel, target_kernel_two),
+        [offsets for _, _, _, offsets, _ in entries],
+    )
+    arrived, matrices = lax.optimization_barrier((arrived, matrices))
+    lines = jnp.concatenate([block[rows : rows + window] for block in (held, arrived)], axis=0)
+    blank = jnp.zeros((whole_tiles(lines.shape[0]) - lines.shape[0], lines.shape[1]), lines.dtype)
+    held = jnp.concatenate([held[:rows], arrived[:rows], lines, blank], axis=0)
     near = [held, *(exchange(held, mask) for mask in last)]
     far = [exchange(part, (0, 0)) for part in near]
     return filter_all(near, far, matrices, entries, groups, window, rows)[:, None]
@@ -544,8 +552,7 @@
         count = lax.axis_size("src")
         fits = (
             lax.axis_size("tgt") == 2
-            and count > 1
-            and count & (count - 1) == 0
+            and count == 8
             and source.shape[1] == 1
             and target.shape[1] == 1
             and cols.shape[0] == count

time: 15.5 us -> 15.4 us (level)
  waiting for transfers between devices: 1.49 us -> 1.16 us
  Pallas kernels: 3.61 us -> 3.79 us
    ppermute x8, waiting for transfers between devices: 1.49 us -> 1.16 us  [exchange(): return lax.ppermute(block, ('src', 'tgt'), pairs)]
    pallas_call x2, Pallas kernels: 1.72 us -> 1.88 us  [from_hbm(): pl.pallas_call(kernel, out_shape=out_shape, in_specs=[pl.BlockSpec(memory...]
  transfers between devices with their start and end apart: 8 -> 8, of which waited for: 4 -> 4; matrix products, arithmetic and copies ran while one was open for 0% -> 0% of each run, Pallas kernels for 8% -> 10%
where the time goes in v1:
time: 15.4 us; the launch traced here: 15.2 us
  starting transfers between devices  10.2 us (66%)
  Pallas kernels  3.79 us (25%)
  waiting for transfers between devices  1.16 us (8%)
    ppermute x8, starting transfers between devices, exchange(): return lax.ppermute(block, ('src', 'tgt'), pairs)  10.2 us
    pallas_call x2, Pallas kernels, local_call(): pl.pallas_call(kernel, out_shape=out_shape, in_specs=[vmem] * len(operand...  1.91 us
    pallas_call x2, Pallas kernels, from_hbm(): pl.pallas_call(kernel, out_shape=out_shape, in_specs=[pl.BlockSpec(memory...  1.88 us
    ppermute x8, waiting for transfers between devices, exchange(): return lax.ppermute(block, ('src', 'tgt'), pairs)  1.16 us
  transfers between devices with their start and end apart: 8, of which 4 were waited for; matrix products, arithmetic and copies ran while one was open for 0% of the time, Pallas kernels for 10%

profile of v1, /device:TPU:0, one launch (start us, length us, event | category | flops | bytes accessed | tf_op | source)
XLA Modules:
  0.0 15.2 jit_solution(2950896798900814978)
XLA Ops:
  0.0 0.8 %shard_map.73 = bf16[40,256]{1,0:T(8,128)(2,1)S(1)} custom-call(s32[4]{0:T(128)} %rows_hbm.1, bf16[32,256]{1,0:T(8,128)(2,1)} %bitcast.5, bf16[32,256]{1,0:T(8,128)(2,1)} %bitcast.6), custom_call_target="tpu_custom_call" | custom-call | tf_op jit(solution)/shard_map/pallas_call | solution.py:77
  0.8 3.6 %collective-permute-start = (bf16[40,256]{1,0:T(8,128)(2,1)S(1)}, bf16[40,256]{1,0:T(8,128)(2,1)S(1)}, u32[]{:S(2)}, u32[]{:S(2)}) collective-permute-start(bf16[40,256]{1,0:T(8,128)(2,1)S(1)} %shard_map.73), channel_id=1, source_target_pairs={{0,9},{1,8},{2,11},{3,10},{4,13},{5,12},{6,15},{7,14},{8,1},{9,0},... | collective-permute-start | bytes 61448 | tf_op jit(solution)/shard_map/ppermute | solution.py:427
  4.4 1.1 %shard_map.74 = (bf16[128,384]{1,0:T(8,128)(2,1)S(1)}, bf16[384,384]{1,0:T(8,128)(2,1)S(1)}, bf16[384,128]{1,0:T(8,128)(2,1)S(1)}) custom-call(s32[8]{0:T(128)} %refs_0_.1, bf16[3,3,16,16]{3,2,1,0:T(8,128)(2,1)} %refs_1_.1, bf16[3,3,16,16]{3,2,1,0:T(8,128)(2,1)} %refs_2_.1, bf16[3,3,16,16]{3,2,1,0:T(8,128)(2,1)} %refs_3_.1), custom_call_target="tpu_custom_call" | custom-call | tf_op jit(solution)/shard_map/pallas_call | solution.py:77
  5.5 0.4 %collective-permute-done = bf16[40,256]{1,0:T(8,128)(2,1)S(1)} collective-permute-done((bf16[40,256]{1,0:T(8,128)(2,1)S(1)}, bf16[40,256]{1,0:T(8,128)(2,1)S(1)}, u32[]{:S(2)}, u32[]{:S(2)}) %collective-permute-start) | collective-permute-done | bytes 20512 | tf_op jit(solution)/shard_map/ppermute | solution.py:427
  5.9 1.8 %collective-permute-start.1 = (bf16[72,256]{1,0:T(8,128)(2,1)S(1)}, bf16[72,256]{1,0:T(8,128)(2,1)S(1)}, u32[]{:S(2)}, u32[]{:S(2)}) collective-permute-start(bf16[72,256]{1,0:T(8,128)(2,1)S(1)} %pad_maximum_fusion.refs_0_), channel_id=1, source_target_pairs={{0,3},{1,4},{2,1},{3,6},{4,7},{5,0},{6,5},{7,2},{8,11},{9,12},{10,... | collective-permute-start | bytes 110600 | tf_op jit(solution)/shard_map/ppermute | solution.py:427
  7.7 0.2 collective-permute-start.2
  7.9 2.6 %collective-permute-start.3 = (bf16[72,256]{1,0:T(8,128)(2,1)S(1)}, bf16[72,256]{1,0:T(8,128)(2,1)S(1)}, u32[]{:S(2)}, u32[]{:S(2)}) collective-permute-start(bf16[72,256]{1,0:T(8,128)(2,1)S(1)} %pad_maximum_fusion.refs_0_), channel_id=1, source_target_pairs={{0,7},{1,6},{2,5},{3,4},{4,3},{5,2},{6,1},{7,0},{8,15},{9,14},{10,... | collective-permute-start | bytes 110600 | tf_op jit(solution)/shard_map/ppermute | solution.py:427
  10.5 0.4 %collective-permute-start.4 = (bf16[72,256]{1,0:T(8,128)(2,1)S(1)}, bf16[72,256]{1,0:T(8,128)(2,1)S(1)}, u32[]{:S(2)}, u32[]{:S(2)}) collective-permute-start(bf16[72,256]{1,0:T(8,128)(2,1)S(1)} %pad_maximum_fusion.refs_0_), channel_id=1, source_target_pairs={{0,1},{1,0},{2,3},{3,2},{4,5},{5,4},{6,7},{7,6},{8,9},{9,8},{10,11... | collective-permute-start | bytes 110600 | tf_op jit(solution)/shard_map/ppermute | solution.py:427
  10.9 0.0 collective-permute-done.1.refs_1_
  10.9 0.1 collective-permute-start.5
  11.0 0.1 collective-permute-done.2.refs_2_
  11.1 0.8 %collective-permute-start.6 = (bf16[72,256]{1,0:T(8,128)(2,1)S(1)}, bf16[72,256]{1,0:T(8,128)(2,1)S(1)}, u32[]{:S(2)}, u32[]{:S(2)}) collective-permute-start(bf16[72,256]{1,0:T(8,128)(2,1)S(1)} %collective-permute-done.2.refs_2_), channel_id=1, source_target_pairs={{0,1},{1,0},{2,3},{3,2},{4,5},{5,4},{6,7},{7,6},{8,9},{9,8},{10,11... | collective-permute-start | bytes 110600 | tf_op jit(solution)/shard_map/ppermute | solution.py:427
  11.9 0.3 %collective-permute-done.3.refs_3_ = bf16[72,256]{1,0:T(8,128)(2,1)S(1)} collective-permute-done((bf16[72,256]{1,0:T(8,128)(2,1)S(1)}, bf16[72,256]{1,0:T(8,128)(2,1)S(1)}, u32[]{:S(2)}, u32[]{:S(2)}) %collective-permute-start.3) | collective-permute-done | bytes 36896 | tf_op jit(solution)/shard_map/ppermute | solution.py:427
  12.1 0.8 %collective-permute-start.7 = (bf16[72,256]{1,0:T(8,128)(2,1)S(1)}, bf16[72,256]{1,0:T(8,128)(2,1)S(1)}, u32[]{:S(2)}, u32[]{:S(2)}) collective-permute-start(bf16[72,256]{1,0:T(8,128)(2,1)S(1)} %collective-permute-done.3.refs_3_), channel_id=1, source_target_pairs={{0,1},{1,0},{2,3},{3,2},{4,5},{5,4},{6,7},{7,6},{8,9},{9,8},{10,11... | collective-permute-start | bytes 110600 | tf_op jit(solution)/shard_map/ppermute | solution.py:427
  12.9 0.0 collective-permute-done.4.refs_4_
  12.9 0.0 collective-permute-done.5.refs_5_
  12.9 0.0 collective-permute-done.6.refs_6_
  12.9 0.5 %shard_map.75 = (bf16[384,128]{1,0:T(8,128)(2,1)S(1)}, f32[96,128]{1,0:T(8,128)S(1)}, bf16[192,256]{1,0:T(8,128)(2,1)S(1)}) custom-call(bf16[72,256]{1,0:T(8,128)(2,1)S(1)} %pad_maximum_fusion.refs_0_, bf16[72,256]{1,0:T(8,128)(2,1)S(1)} %collective-permute-done.1.refs_1_, bf16[72,256]{1,0:T(8,128)(2,1)S(1)} %collective-permute-done.2.refs_2_, ...), custom_call_target="tpu_custom_call" | custom-call | tf_op jit(solution)/shard_map/pallas_call | solution.py:376
  13.4 0.4 %collective-permute-done.7.last_ref = bf16[72,256]{1,0:T(8,128)(2,1)S(1)} collective-permute-done((bf16[72,256]{1,0:T(8,128)(2,1)S(1)}, bf16[72,256]{1,0:T(8,128)(2,1)S(1)}, u32[]{:S(2)}, u32[]{:S(2)}) %collective-permute-start.7) | collective-permute-done | bytes 36896 | tf_op jit(solution)/shard_map/ppermute | solution.py:427
  13.8 1.4 %shard_map.76 = bf16[4,32,128]{2,1,0:T(8,128)(2,1)} custom-call(bf16[384,128]{1,0:T(8,128)(2,1)S(1)} %get-tuple-element.19.base_ref, f32[96,128]{1,0:T(8,128)S(1)} %get-tuple-element.20.edge_ref, bf16[192,256]{1,0:T(8,128)(2,1)S(1)} %get-tuple-element.21.spread_ref, bf16[72,256]{1,0:T(8,128)(2,1)S(1)} %collective-permute-done.7.last_ref, ...), custom_call_target="tpu_custom_call" | custom-call | tf_op jit(solution)/shard_map/pallas_call | solution.py:376
  (5 shorter events, 0.0 us)
Async XLA Ops:
  0.8 5.1 %collective-permute-start = (bf16[40,256]{1,0:T(8,128)(2,1)S(1)}, bf16[40,256]{1,0:T(8,128)(2,1)S(1)}, u32[]{:S(2)}, u32[]{:S(2)}) collective-permute-start(bf16[40,256]{1,0:T(8,128)(2,1)S(1)} %shard_map.73), channel_id=1, source_target_pairs={{0,9},{1,8},{2,11},{3,10},{4,13},{5,12},{6,15},{7,14},{8,1},{9,0},... | collective-permute-start | bytes 61448 | tf_op jit(solution)/shard_map/ppermute | solution.py:427
  5.9 5.0 %collective-permute-start.1 = (bf16[72,256]{1,0:T(8,128)(2,1)S(1)}, bf16[72,256]{1,0:T(8,128)(2,1)S(1)}, u32[]{:S(2)}, u32[]{:S(2)}) collective-permute-start(bf16[72,256]{1,0:T(8,128)(2,1)S(1)} %pad_maximum_fusion.refs_0_), channel_id=1, source_target_pairs={{0,3},{1,4},{2,1},{3,6},{4,7},{5,0},{6,5},{7,2},{8,11},{9,12},{10,... | collective-permute-start | bytes 110600 | tf_op jit(solution)/shard_map/ppermute | solution.py:427
  7.7 3.4 %collective-permute-start.2 = (bf16[72,256]{1,0:T(8,128)(2,1)S(1)}, bf16[72,256]{1,0:T(8,128)(2,1)S(1)}, u32[]{:S(2)}, u32[]{:S(2)}) collective-permute-start(bf16[72,256]{1,0:T(8,128)(2,1)S(1)} %pad_maximum_fusion.refs_0_), channel_id=1, source_target_pairs={{0,5},{1,2},{2,7},{3,0},{4,1},{5,6},{6,3},{7,4},{8,13},{9,10},{10,... | collective-permute-start | bytes 110600 | tf_op jit(solution)/shard_map/ppermute | solution.py:427
  7.9 4.3 %collective-permute-start.3 = (bf16[72,256]{1,0:T(8,128)(2,1)S(1)}, bf16[72,256]{1,0:T(8,128)(2,1)S(1)}, u32[]{:S(2)}, u32[]{:S(2)}) collective-permute-start(bf16[72,256]{1,0:T(8,128)(2,1)S(1)} %pad_maximum_fusion.refs_0_), channel_id=1, source_target_pairs={{0,7},{1,6},{2,5},{3,4},{4,3},{5,2},{6,1},{7,0},{8,15},{9,14},{10,... | collective-permute-start | bytes 110600 | tf_op jit(solution)/shard_map/ppermute | solution.py:427
  10.5 2.4 %collective-permute-start.4 = (bf16[72,256]{1,0:T(8,128)(2,1)S(1)}, bf16[72,256]{1,0:T(8,128)(2,1)S(1)}, u32[]{:S(2)}, u32[]{:S(2)}) collective-permute-start(bf16[72,256]{1,0:T(8,128)(2,1)S(1)} %pad_maximum_fusion.refs_0_), channel_id=1, source_target_pairs={{0,1},{1,0},{2,3},{3,2},{4,5},{5,4},{6,7},{7,6},{8,9},{9,8},{10,11... | collective-permute-start | bytes 110600 | tf_op jit(solution)/shard_map/ppermute | solution.py:427
  10.9 2.0 %collective-permute-start.5 = (bf16[72,256]{1,0:T(8,128)(2,1)S(1)}, bf16[72,256]{1,0:T(8,128)(2,1)S(1)}, u32[]{:S(2)}, u32[]{:S(2)}) collective-permute-start(bf16[72,256]{1,0:T(8,128)(2,1)S(1)} %collective-permute-done.1.refs_1_), channel_id=1, source_target_pairs={{0,1},{1,0},{2,3},{3,2},{4,5},{5,4},{6,7},{7,6},{8,9},{9,8},{10,11... | collective-permute-start | bytes 110600 | tf_op jit(solution)/shard_map/ppermute | solution.py:427
  11.1 1.8 %collective-permute-start.6 = (bf16[72,256]{1,0:T(8,128)(2,1)S(1)}, bf16[72,256]{1,0:T(8,128)(2,1)S(1)}, u32[]{:S(2)}, u32[]{:S(2)}) collective-permute-start(bf16[72,256]{1,0:T(8,128)(2,1)S(1)} %collective-permute-done.2.refs_2_), channel_id=1, source_target_pairs={{0,1},{1,0},{2,3},{3,2},{4,5},{5,4},{6,7},{7,6},{8,9},{9,8},{10,11... | collective-permute-start | bytes 110600 | tf_op jit(solution)/shard_map/ppermute | solution.py:427
  12.1 1.6 %collective-permute-start.7 = (bf16[72,256]{1,0:T(8,128)(2,1)S(1)}, bf16[72,256]{1,0:T(8,128)(2,1)S(1)}, u32[]{:S(2)}, u32[]{:S(2)}) collective-permute-start(bf16[72,256]{1,0:T(8,128)(2,1)S(1)} %collective-permute-done.3.refs_3_), channel_id=1, source_target_pairs={{0,1},{1,0},{2,3},{3,2},{4,5},{5,4},{6,7},{7,6},{8,9},{9,8},{10,11... | collective-permute-start | bytes 110600 | tf_op jit(solution)/shard_map/ppermute | solution.py:427
